TPU v7x, 32 devices: a whole 2x2x4 slice. The times are simulated.
32 devices in a mesh: prow: 8 (over y, x, core), pcol: 4 (over z).
Axes of the slice: x: 2, y: 2, z: 4, core: 2. Of those that a mesh axis runs over, the one named last changes fastest.
Arguments:
- panel: float32 [16, 1024, 128], P('pcol', 'prow'), may hold values from -8 to 192, as said below
- strip: float32 [16, 1024, 2, 512], P(None, 'prow', None, 'pcol'), may hold values from -6 to 6
- factor: float32 [16, 1024, 2, 512], P(None, 'prow', None, 'pcol'), may hold values from -0.125 to 0.125
- inv_diag: float32 [8, 128, 128], replicated, may hold values from -0.24 to 1.4, as said below
- rhs: float32 [16, 1024, 256], P(None, 'prow'), may hold values from -6 to 6
Outputs:
- panel_factor: float32 [16, 1024, 128], P('pcol', 'prow')
- new_strip: float32 [16, 1024, 2, 512], P(None, 'prow', None, 'pcol')
- forward: float32 [16, 1024, 256], P(None, 'prow')
Inputs may be any that keep to these rules, and one draw needn't show every extreme that they name: Row tile 8 of the panel, read as in the first step, is symmetric positive definite. `inv_diag`: every block is lower triangular with a positive diagonal.
All inputs are finite; a program needn't handle non-finite values.
Results may differ from a plain program's by a relative error of at most 0.00018.
Values sent between devices are 32-bit elements; how exact they have to be, the bound alone decides.
A program may use at most 64 MiB of HBM per device.

v0:
```python
import jax
import jax.numpy as jnp
from jax import lax
from jax.sharding import PartitionSpec as P

KF = 2
CTD = 2


def from_root(block, axis, owner):
    block = jnp.where(lax.axis_index(axis) == owner, block, jnp.zeros_like(block))
    return lax.psum(block, axis)


def per_device(panel, strip, factor, inv_diag, rhs):
    highest = lax.Precision.HIGHEST
    grid_rows = lax.axis_size("prow")
    grid_cols = lax.axis_size("pcol")
    row_place = lax.axis_index("prow")
    col_place = lax.axis_index("pcol")
    own_tiles = panel.shape[0]
    tile_size = panel.shape[1]
    tile_rows = strip.shape[0]
    rhs_count = rhs.shape[2]
    sweep_tiles = KF * grid_cols
    strip_tiles = CTD * grid_cols
    diag_row = sweep_tiles // grid_rows
    root_index = sweep_tiles % grid_rows * grid_cols + diag_row // own_tiles
    diag_block = from_root(panel[diag_row % own_tiles], ("prow", "pcol"), root_index)
    diag_factor = jnp.linalg.cholesky(diag_block)
    inverse = jax.scipy.linalg.solve_triangular(
        diag_factor, jnp.eye(tile_size, dtype=jnp.float32), lower=True
    )
    scaled = jnp.einsum("atb,cb->atc", panel, inverse, precision=highest)
    local_tile = (col_place * own_tiles + jnp.arange(own_tiles)) * grid_rows + row_place
    panel_factor = jnp.where((local_tile > sweep_tiles)[:, None, None], scaled, 0.0)
    panel_factor = jnp.where(
        (local_tile == sweep_tiles)[:, None, None], diag_factor[None], panel_factor
    )
    row_factor = lax.all_gather(panel_factor, "pcol", axis=0, tiled=True)
    row_tile = jnp.arange(tile_rows) * grid_rows + row_place
    below_part = jnp.where((row_tile > sweep_tiles)[:, None, None], row_factor, 0.0)
    wanted = sweep_tiles + 1 + jnp.arange(CTD) * grid_cols + col_place
    slot_count = -(-strip_tiles // grid_rows)
    first_slot = (sweep_tiles + grid_rows - row_place) // grid_rows
    outgoing = lax.dynamic_slice_in_dim(below_part, first_slot, slot_count, 0)
    pooled = lax.all_gather(outgoing, "prow", axis=0, tiled=True)
    owner_row = wanted % grid_rows
    slot_place = (
        owner_row * slot_count
        + wanted // grid_rows
        - (sweep_tiles + grid_rows - owner_row) // grid_rows
    )
    column = pooled[slot_place]
    new_strip = strip - jnp.einsum("itb,scb->itsc", below_part, column, precision=highest)
    start_solved = jnp.zeros((sweep_tiles, tile_size, rhs_count), jnp.float32)
    reduce_row = lambda pending: lax.psum(pending, "pcol")
    spread_row = lambda solution, root_row: from_root(solution, "prow", root_row)

    def advance(sweep_step, carried):
        partial_rows, solved, pending = carried
        tile_here = sweep_step // grid_rows
        pending = lax.dynamic_index_in_dim(partial_rows, tile_here, 0, keepdims=False)
        summed = reduce_row(pending)
        residue = lax.dynamic_index_in_dim(rhs, tile_here, 0, keepdims=False) - summed
        diag_inverse = lax.dynamic_index_in_dim(inv_diag, sweep_step, 0, keepdims=False)
        solution = jnp.dot(diag_inverse, residue, precision=highest)
        solution = spread_row(solution, sweep_step % grid_rows)
        solved = lax.dynamic_update_index_in_dim(solved, solution, sweep_step, 0)
        columns = lax.dynamic_index_in_dim(factor, sweep_step // grid_cols, 2, keepdims=False)
        holds_column = col_place == sweep_step % grid_cols
        update = jnp.einsum("itc,cr->itr", columns, solution, precision=highest)
        partial_rows = partial_rows + jnp.where(holds_column, update, 0.0)
        return (partial_rows, solved, pending)

    start_rows = jnp.zeros(rhs.shape, jnp.float32)
    start_pending = jnp.zeros((tile_size, rhs_count), jnp.float32)
    partial_rows, solved, unused_pending = lax.fori_loop(
        0, sweep_tiles, advance, (start_rows, start_solved, start_pending)
    )
    partial_rows, solved = (partial_rows, solved)
    totals = lax.psum(partial_rows, "pcol")
    remains = rhs - totals
    panel_solution = jnp.dot(inverse, remains[sweep_tiles // grid_rows], precision=highest)
    panel_solution = from_root(panel_solution, "prow", sweep_tiles % grid_rows)
    remains = remains - jnp.einsum("itb,br->itr", below_part, panel_solution, precision=highest)
    earlier = solved[jnp.minimum(row_tile, sweep_tiles - 1)]
    forward = jnp.where((row_tile == sweep_tiles)[:, None, None], panel_solution[None], remains)
    forward = jnp.where((row_tile < sweep_tiles)[:, None, None], earlier, forward)
    return (panel_factor, new_strip, forward)


def solution(mesh):
    in_specs = (
        P("pcol", "prow", None),
        P(None, "prow", None, "pcol"),
        P(None, "prow", None, "pcol"),
        P(),
        P(None, "prow", None),
    )
    out_specs = (P("pcol", "prow", None), P(None, "prow", None, "pcol"), P(None, "prow", None))
    return jax.shard_map(
        per_device, mesh=mesh, in_specs=in_specs, out_specs=out_specs, check_vma=False
    )
```

profile of v0, /device:TPU:0, one launch (start us, length us, event | category | flops | bytes accessed | tf_op | source)
XLA Modules:
  0.0 1144.2 jit_solution(4040450262911026411)
XLA Ops:
  8.9 125.6 %all-reduce.6.cloned.1.call-done = f32[128,128]{0,1:T(8,128)} async-done(((f32[128,128]{0,1:T(8,128)}), f32[128,128]{0,1:T(8,128)}) %all-reduce.6.cloned.1.call-update) | async-done | bytes 65552 | tf_op jit(solution)/shard_map/psum | solution.py:12
  136.2 11.7 %cholesky.19 = f32[128,128]{1,0:T(8,128)S(1)} custom-call(f32[128,128]{1,0:T(8,128)S(1)} %fusion.13), custom_call_target="Cholesky" | custom-call | tf_op jit(solution)/shard_map/jit(cholesky)/cholesky | solution.py:30
  149.3 9.8 custom-call.7
  161.6 796.4 %while.19 = (s32[]{:T(128)}, f32[16,128,256]{2,1,0:T(8,128)}, f32[8,128,256]{2,1,0:T(8,128)}, s32[]{:T(128)}, f32[16,128,2,128]{3,2,1,0:T(2,128)}, /*index=5*/f3...) while((s32[]{:T(128)}, f32[16,128,256]{2,1,0:T(8,128)}, ...), condition=%wide.region_6.7_spmd.clone, body=%wide.region_3.6_spmd.clone.sunk | while | flops 857342016 | bytes 14221928 | solution.py:78
  162.6 38.0 %all-reduce.12.cloned.1.call-done = f32[128,256]{1,0:T(8,128)} async-done(((f32[128,256]{1,0:T(8,128)}), f32[128,256]{1,0:T(8,128)}) %all-reduce.12.cloned.1.call-update) | async-done | bytes 131088 | tf_op jit(solution)/shard_map/while/body/eval_jaxpr/psum | solution.py:57
  200.7 1.9 convolution_select_fusion.4
  202.6 2.7 constant_dynamic-slice_fusion.3
  205.3 51.9 %all-reduce.14.cloned.1.call-done = f32[128,256]{1,0:T(8,128)} async-done(((f32[128,256]{1,0:T(8,128)}), f32[128,256]{1,0:T(8,128)}) %all-reduce.14.cloned.1.call-update) | async-done | bytes 131088 | tf_op jit(solution)/shard_map/while/body/eval_jaxpr/psum | solution.py:12
  258.7 4.0 select_add_fusion.2
  265.3 34.7 %all-reduce.12.cloned.1.call-done = f32[128,256]{1,0:T(8,128)} async-done(((f32[128,256]{1,0:T(8,128)}), f32[128,256]{1,0:T(8,128)}) %all-reduce.12.cloned.1.call-update) | async-done | bytes 131088 | tf_op jit(solution)/shard_map/while/body/eval_jaxpr/psum | solution.py:57
  300.0 1.9 convolution_select_fusion.4
  302.0 2.7 constant_dynamic-slice_fusion.3
  304.7 51.7 %all-reduce.14.cloned.1.call-done = f32[128,256]{1,0:T(8,128)} async-done(((f32[128,256]{1,0:T(8,128)}), f32[128,256]{1,0:T(8,128)}) %all-reduce.14.cloned.1.call-update) | async-done | bytes 131088 | tf_op jit(solution)/shard_map/while/body/eval_jaxpr/psum | solution.py:12
  357.9 4.0 select_add_fusion.2
  364.5 34.7 %all-reduce.12.cloned.1.call-done = f32[128,256]{1,0:T(8,128)} async-done(((f32[128,256]{1,0:T(8,128)}), f32[128,256]{1,0:T(8,128)}) %all-reduce.12.cloned.1.call-update) | async-done | bytes 131088 | tf_op jit(solution)/shard_map/while/body/eval_jaxpr/psum | solution.py:57
  401.2 2.7 constant_dynamic-slice_fusion.3
  403.9 51.9 %all-reduce.14.cloned.1.call-done = f32[128,256]{1,0:T(8,128)} async-done(((f32[128,256]{1,0:T(8,128)}), f32[128,256]{1,0:T(8,128)}) %all-reduce.14.cloned.1.call-update) | async-done | bytes 131088 | tf_op jit(solution)/shard_map/while/body/eval_jaxpr/psum | solution.py:12
  457.3 4.0 select_add_fusion.2
  463.9 35.0 %all-reduce.12.cloned.1.call-done = f32[128,256]{1,0:T(8,128)} async-done(((f32[128,256]{1,0:T(8,128)}), f32[128,256]{1,0:T(8,128)}) %all-reduce.12.cloned.1.call-update) | async-done | bytes 131088 | tf_op jit(solution)/shard_map/while/body/eval_jaxpr/psum | solution.py:57
  500.8 2.7 constant_dynamic-slice_fusion.3
  503.5 51.9 %all-reduce.14.cloned.1.call-done = f32[128,256]{1,0:T(8,128)} async-done(((f32[128,256]{1,0:T(8,128)}), f32[128,256]{1,0:T(8,128)}) %all-reduce.14.cloned.1.call-update) | async-done | bytes 131088 | tf_op jit(solution)/shard_map/while/body/eval_jaxpr/psum | solution.py:12
  557.0 4.0 select_add_fusion.2
  563.6 34.6 %all-reduce.12.cloned.1.call-done = f32[128,256]{1,0:T(8,128)} async-done(((f32[128,256]{1,0:T(8,128)}), f32[128,256]{1,0:T(8,128)}) %all-reduce.12.cloned.1.call-update) | async-done | bytes 131088 | tf_op jit(solution)/shard_map/while/body/eval_jaxpr/psum | solution.py:57
  600.1 2.7 constant_dynamic-slice_fusion.3
  602.8 51.9 %all-reduce.14.cloned.1.call-done = f32[128,256]{1,0:T(8,128)} async-done(((f32[128,256]{1,0:T(8,128)}), f32[128,256]{1,0:T(8,128)}) %all-reduce.14.cloned.1.call-update) | async-done | bytes 131088 | tf_op jit(solution)/shard_map/while/body/eval_jaxpr/psum | solution.py:12
  656.3 4.0 select_add_fusion.2
  662.9 34.7 %all-reduce.12.cloned.1.call-done = f32[128,256]{1,0:T(8,128)} async-done(((f32[128,256]{1,0:T(8,128)}), f32[128,256]{1,0:T(8,128)}) %all-reduce.12.cloned.1.call-update) | async-done | bytes 131088 | tf_op jit(solution)/shard_map/while/body/eval_jaxpr/psum | solution.py:57
  697.6 1.9 convolution_select_fusion.4
  699.5 2.7 constant_dynamic-slice_fusion.3
  702.2 51.9 %all-reduce.14.cloned.1.call-done = f32[128,256]{1,0:T(8,128)} async-done(((f32[128,256]{1,0:T(8,128)}), f32[128,256]{1,0:T(8,128)}) %all-reduce.14.cloned.1.call-update) | async-done | bytes 131088 | tf_op jit(solution)/shard_map/while/body/eval_jaxpr/psum | solution.py:12
  755.6 4.0 select_add_fusion.2
  762.2 34.6 %all-reduce.12.cloned.1.call-done = f32[128,256]{1,0:T(8,128)} async-done(((f32[128,256]{1,0:T(8,128)}), f32[128,256]{1,0:T(8,128)}) %all-reduce.12.cloned.1.call-update) | async-done | bytes 131088 | tf_op jit(solution)/shard_map/while/body/eval_jaxpr/psum | solution.py:57
  798.8 2.7 constant_dynamic-slice_fusion.3
  801.5 51.7 %all-reduce.14.cloned.1.call-done = f32[128,256]{1,0:T(8,128)} async-done(((f32[128,256]{1,0:T(8,128)}), f32[128,256]{1,0:T(8,128)}) %all-reduce.14.cloned.1.call-update) | async-done | bytes 131088 | tf_op jit(solution)/shard_map/while/body/eval_jaxpr/psum | solution.py:12
  854.8 4.0 select_add_fusion.2
  861.4 34.7 %all-reduce.12.cloned.1.call-done = f32[128,256]{1,0:T(8,128)} async-done(((f32[128,256]{1,0:T(8,128)}), f32[128,256]{1,0:T(8,128)}) %all-reduce.12.cloned.1.call-update) | async-done | bytes 131088 | tf_op jit(solution)/shard_map/while/body/eval_jaxpr/psum | solution.py:57
  898.0 2.7 constant_dynamic-slice_fusion.3
  900.7 51.7 %all-reduce.14.cloned.1.call-done = f32[128,256]{1,0:T(8,128)} async-done(((f32[128,256]{1,0:T(8,128)}), f32[128,256]{1,0:T(8,128)}) %all-reduce.14.cloned.1.call-update) | async-done | bytes 131088 | tf_op jit(solution)/shard_map/while/body/eval_jaxpr/psum | solution.py:12
  954.0 4.0 select_add_fusion.2
  959.4 2.0 gather_fusion.1
  961.5 26.5 %all-gather.2.cloned.1.call-done = f32[16,128,128]{2,1,0:T(8,128)} async-done(((f32[4,128,128]{2,1,0:T(8,128)}), f32[16,128,128]{2,1,0:T(8,128)}) %all-gather.2.cloned.1.call-update) | async-done | bytes 1048592 | tf_op jit(solution)/shard_map/all_gather | solution.py:40
  989.4 10.0 all_gather.7
  1000.0 77.0 %all-reduce.8.cloned.1.call-done = f32[16,128,256]{2,1,0:T(8,128)} async-done(((f32[16,128,256]{2,1,0:T(8,128)}), f32[16,128,256]{2,1,0:T(8,128)}) %all-reduce.8.cloned.1.call-update) | async-done | bytes 2097168 | tf_op jit(solution)/shard_map/psum | solution.py:82
  1077.0 2.5 sub.72
  1080.5 3.4 copy_subtract_fusion
  1083.9 2.9 copy.25
  1086.8 45.9 %all-reduce.10.cloned.1.call-done = f32[128,256]{1,0:T(8,128)} async-done(((f32[128,256]{1,0:T(8,128)}), f32[128,256]{1,0:T(8,128)}) %all-reduce.10.cloned.1.call-update) | async-done | bytes 131088 | tf_op jit(solution)/shard_map/psum | solution.py:12
  1132.7 4.7 select_select_fusion
  (96 shorter events, 52.5 us)
Async XLA Ops:
  7.2 127.3 %all-reduce.6.cloned.1.call-start = ((), (), s32[]{:S(2)}) async-start(), calls=%async_computation | async-start | bytes 131072 | tf_op jit(solution)/shard_map/psum | solution.py:12
  161.6 39.0 %all-reduce.12.cloned.1.call-start = ((), (), s32[]{:S(2)}) async-start(), calls=%async_computation.4 | async-start | bytes 262144 | tf_op jit(solution)/shard_map/while/body/eval_jaxpr/psum | solution.py:57
  162.6 94.6 %all-reduce.14.cloned.1.call-start = ((), (), s32[]{:S(2)}) async-start(), calls=%async_computation.5 | async-start | bytes 262144 | tf_op jit(solution)/shard_map/while/body/eval_jaxpr/psum | solution.py:12
  262.7 37.3 %all-reduce.12.cloned.1.call-start = ((), (), s32[]{:S(2)}) async-start(), calls=%async_computation.4 | async-start | bytes 262144 | tf_op jit(solution)/shard_map/while/body/eval_jaxpr/psum | solution.py:57
  265.3 91.1 %all-reduce.14.cloned.1.call-start = ((), (), s32[]{:S(2)}) async-start(), calls=%async_computation.5 | async-start | bytes 262144 | tf_op jit(solution)/shard_map/while/body/eval_jaxpr/psum | solution.py:12
  361.9 37.3 %all-reduce.12.cloned.1.call-start = ((), (), s32[]{:S(2)}) async-start(), calls=%async_computation.4 | async-start | bytes 262144 | tf_op jit(solution)/shard_map/while/body/eval_jaxpr/psum | solution.py:57
  364.5 91.3 %all-reduce.14.cloned.1.call-start = ((), (), s32[]{:S(2)}) async-start(), calls=%async_computation.5 | async-start | bytes 262144 | tf_op jit(solution)/shard_map/while/body/eval_jaxpr/psum | solution.py:12
  461.3 37.5 %all-reduce.12.cloned.1.call-start = ((), (), s32[]{:S(2)}) async-start(), calls=%async_computation.4 | async-start | bytes 262144 | tf_op jit(solution)/shard_map/while/body/eval_jaxpr/psum | solution.py:57
  463.8 91.6 %all-reduce.14.cloned.1.call-start = ((), (), s32[]{:S(2)}) async-start(), calls=%async_computation.5 | async-start | bytes 262144 | tf_op jit(solution)/shard_map/while/body/eval_jaxpr/psum | solution.py:12
  561.0 37.2 %all-reduce.12.cloned.1.call-start = ((), (), s32[]{:S(2)}) async-start(), calls=%async_computation.4 | async-start | bytes 262144 | tf_op jit(solution)/shard_map/while/body/eval_jaxpr/psum | solution.py:57
  563.5 91.2 %all-reduce.14.cloned.1.call-start = ((), (), s32[]{:S(2)}) async-start(), calls=%async_computation.5 | async-start | bytes 262144 | tf_op jit(solution)/shard_map/while/body/eval_jaxpr/psum | solution.py:12
  660.3 37.3 %all-reduce.12.cloned.1.call-start = ((), (), s32[]{:S(2)}) async-start(), calls=%async_computation.4 | async-start | bytes 262144 | tf_op jit(solution)/shard_map/while/body/eval_jaxpr/psum | solution.py:57
  662.8 91.3 %all-reduce.14.cloned.1.call-start = ((), (), s32[]{:S(2)}) async-start(), calls=%async_computation.5 | async-start | bytes 262144 | tf_op jit(solution)/shard_map/while/body/eval_jaxpr/psum | solution.py:12
  759.6 37.2 %all-reduce.12.cloned.1.call-start = ((), (), s32[]{:S(2)}) async-start(), calls=%async_computation.4 | async-start | bytes 262144 | tf_op jit(solution)/shard_map/while/body/eval_jaxpr/psum | solution.py:57
  762.2 91.1 %all-reduce.14.cloned.1.call-start = ((), (), s32[]{:S(2)}) async-start(), calls=%async_computation.5 | async-start | bytes 262144 | tf_op jit(solution)/shard_map/while/body/eval_jaxpr/psum | solution.py:12
  858.8 37.3 %all-reduce.12.cloned.1.call-start = ((), (), s32[]{:S(2)}) async-start(), calls=%async_computation.4 | async-start | bytes 262144 | tf_op jit(solution)/shard_map/while/body/eval_jaxpr/psum | solution.py:57
  861.3 91.1 %all-reduce.14.cloned.1.call-start = ((), (), s32[]{:S(2)}) async-start(), calls=%async_computation.5 | async-start | bytes 262144 | tf_op jit(solution)/shard_map/while/body/eval_jaxpr/psum | solution.py:12
  958.0 1.4 copy-start
  958.0 30.0 %all-gather.2.cloned.1.call-start = ((), (), s32[]{:S(2)}) async-start(), calls=%async_computation.1 | async-start | bytes 1310720 | tf_op jit(solution)/shard_map/all_gather | solution.py:40
  958.6 118.4 %all-reduce.8.cloned.1.call-start = ((), (), s32[]{:S(2)}) async-start(), calls=%async_computation.2 | async-start | bytes 4194304 | tf_op jit(solution)/shard_map/psum | solution.py:82
  959.3 173.4 %all-reduce.10.cloned.1.call-start = ((), (), s32[]{:S(2)}) async-start(), calls=%async_computation.3 | async-start | bytes 262144 | tf_op jit(solution)/shard_map/psum | solution.py:12
Sparse Core Ops, SparseCore 0:
  14.2 120.2 all-reduce.5
  165.4 35.2 all-reduce.11
  204.6 52.5 all-reduce.13
  266.1 33.8 all-reduce.11
  303.8 52.5 all-reduce.13
  365.3 33.8 all-reduce.11
  403.1 52.5 all-reduce.13
  465.0 33.7 all-reduce.11
  502.8 52.5 all-reduce.13
  564.4 33.7 all-reduce.11
  602.1 52.5 all-reduce.13
  663.7 33.8 all-reduce.11
  701.5 52.5 all-reduce.13
  763.0 33.7 all-reduce.11
  800.6 52.5 all-reduce.13
  862.2 33.8 all-reduce.11
  899.8 52.5 all-reduce.13
  960.7 27.2 all-gather.1
  990.9 86.0 all-reduce.7
  1080.7 51.9 all-reduce.9
where the time goes:
time: 1150 us; the launch traced here: 1140 us
  waiting for transfers between devices  972 us (85%)
  matrix products  58 us (5%)
  local copies, waits for them, and re-layouts  47.7 us (4%)
  other arithmetic  41.2 us (4%)
  between operations  14.2 us (1%)
    psum x10, waiting for transfers between devices, from_root(): return lax.psum(block, axis)  586 us
    psum x8, waiting for transfers between devices, per_device(): reduce_row = lambda pending: lax.psum(pending, 'pcol')  281 us
    psum x1, waiting for transfers between devices, per_device(): totals = lax.psum(partial_rows, 'pcol')  77 us
    dot_general x8, matrix products, advance(): update = jnp.einsum('itc,cr->itr', columns, solution, precision=highest)  32.1 us
    all_gather x1, waiting for transfers between devices, per_device(): row_factor = lax.all_gather(panel_factor, 'pcol', axis=0, tiled=True)  26.5 us
  transfers between devices with their start and end apart: 20, of which 20 were waited for; matrix products, arithmetic and copies ran while one was open for 3% of the time, Pallas kernels for 0%

commit v1 on v0

--- a/solution.py
+++ b/solution.py
@@ -9,7 +9,7 @@
 
 def from_root(block, axis, owner):
     block = jnp.where(lax.axis_index(axis) == owner, block, jnp.zeros_like(block))
-    return lax.psum(block, axis)
+    return jnp.sum(lax.all_gather(block, axis), axis=0)
 
 
 def per_device(panel, strip, factor, inv_diag, rhs):

time: 1150 us -> 760 us (0.66)
  waiting for transfers between devices: 972 us -> 587 us
  other arithmetic: 41.2 us -> 54.6 us
    psum x10 -> x0, waiting for transfers between devices: 586 us -> none  [from_root(): return lax.psum(block, axis)]
    all_gather x0 -> x10, waiting for transfers between devices: none -> 274 us  [from_root(): return jnp.sum(lax.all_gather(block, axis), axis=0)]
    psum x1, waiting for transfers between devices: 77 us -> 0.02 us  [per_device(): totals = lax.psum(partial_rows, 'pcol')]
    reduce_sum x0 -> x10, other arithmetic: none -> 13.4 us  [from_root(): return jnp.sum(lax.all_gather(block, axis), axis=0)]
  transfers between devices with their start and end apart: 20 -> 20, of which waited for: 20 -> 19; matrix products, arithmetic and copies ran while one was open for 3% -> 8% of each run, Pallas kernels for 0% -> 0%
where the time goes in v1:
time: 760 us; the launch traced here: 758 us
  waiting for transfers between devices  587 us (77%)
  other arithmetic  54.6 us (7%)
  matrix products  49.9 us (7%)
  local copies, waits for them, and re-layouts  39.8 us (5%)
  between operations  15.4 us (2%)
  blocking collectives  11 us (1%)
    psum x8, waiting for transfers between devices, per_device(): reduce_row = lambda pending: lax.psum(pending, 'pcol')  289 us
    all_gather x10, waiting for transfers between devices, from_root(): return jnp.sum(lax.all_gather(block, axis), axis=0)  274 us
    dot_general x8, matrix products, advance(): update = jnp.einsum('itc,cr->itr', columns, solution, precision=highest)  24.9 us
    dynamic_slice x8, local copies, waits for them, and re-layouts, advance(): lax.dynamic_index_in_dim(factor, sweep_step // grid_cols, 2, keepdims=False)  21.5 us
    all_gather x1, waiting for transfers between devices, per_device(): row_factor = lax.all_gather(panel_factor, 'pcol', axis=0, tiled=True)  21.4 us
    dot_general x8, matrix products, advance(): solution = jnp.dot(diag_inverse, residue, precision=highest)  15.4 us
  transfers between devices with their start and end apart: 20, of which 19 were waited for; matrix products, arithmetic and copies ran while one was open for 8% of the time, Pallas kernels for 0%

profile of v1, /device:TPU:0, one launch (start us, length us, event | category | flops | bytes accessed | tf_op | source)
XLA Modules:
  0.0 758.3 jit_solution(8417935347485946068)
XLA Ops:
  9.5 553.3 %while.19 = (s32[]{:T(128)}, f32[16,128,256]{2,1,0:T(8,128)}, f32[8,128,256]{2,1,0:T(8,128)}, s32[]{:T(128)}, f32[16,128,2,128]{3,2,1,0:T(2,128)}, /*index=5*/f3...) while((s32[]{:T(128)}, f32[16,128,256]{2,1,0:T(8,128)}, ...), condition=%wide.region_6.7_spmd.clone, body=%wide.region_3.6_spmd.clone.sunk | while | flops 857538624 | bytes 18154100 | solution.py:78
  10.5 40.0 %all-reduce.5.cloned.1.call-done = f32[128,256]{1,0:T(8,128)} async-done(((f32[128,256]{1,0:T(8,128)}), f32[128,256]{1,0:T(8,128)}) %all-reduce.5.cloned.1.call-update) | async-done | bytes 131088 | tf_op jit(solution)/shard_map/while/body/eval_jaxpr/psum | solution.py:57
  52.5 2.7 constant_dynamic-slice_fusion.3
  55.2 21.0 %all-gather.16.cloned.1.call-done = f32[1024,256]{1,0:T(8,128)} async-done(((f32[128,256]{1,0:T(8,128)}), f32[1024,256]{1,0:T(8,128)}) %all-gather.16.cloned.1.call-update) | async-done | bytes 1048592 | tf_op jit(solution)/shard_map/while/body/eval_jaxpr/all_gather | solution.py:12
  78.1 3.1 select_add_fusion.2
  83.8 35.7 %all-reduce.5.cloned.1.call-done = f32[128,256]{1,0:T(8,128)} async-done(((f32[128,256]{1,0:T(8,128)}), f32[128,256]{1,0:T(8,128)}) %all-reduce.5.cloned.1.call-update) | async-done | bytes 131088 | tf_op jit(solution)/shard_map/while/body/eval_jaxpr/psum | solution.py:57
  121.5 2.7 constant_dynamic-slice_fusion.3
  124.2 20.8 %all-gather.16.cloned.1.call-done = f32[1024,256]{1,0:T(8,128)} async-done(((f32[128,256]{1,0:T(8,128)}), f32[1024,256]{1,0:T(8,128)}) %all-gather.16.cloned.1.call-update) | async-done | bytes 1048592 | tf_op jit(solution)/shard_map/while/body/eval_jaxpr/all_gather | solution.py:12
  147.0 3.1 select_add_fusion.2
  152.7 35.4 %all-reduce.5.cloned.1.call-done = f32[128,256]{1,0:T(8,128)} async-done(((f32[128,256]{1,0:T(8,128)}), f32[128,256]{1,0:T(8,128)}) %all-reduce.5.cloned.1.call-update) | async-done | bytes 131088 | tf_op jit(solution)/shard_map/while/body/eval_jaxpr/psum | solution.py:57
  190.0 2.7 constant_dynamic-slice_fusion.3
  192.7 20.8 %all-gather.16.cloned.1.call-done = f32[1024,256]{1,0:T(8,128)} async-done(((f32[128,256]{1,0:T(8,128)}), f32[1024,256]{1,0:T(8,128)}) %all-gather.16.cloned.1.call-update) | async-done | bytes 1048592 | tf_op jit(solution)/shard_map/while/body/eval_jaxpr/all_gather | solution.py:12
  215.5 3.1 select_add_fusion.2
  221.2 35.7 %all-reduce.5.cloned.1.call-done = f32[128,256]{1,0:T(8,128)} async-done(((f32[128,256]{1,0:T(8,128)}), f32[128,256]{1,0:T(8,128)}) %all-reduce.5.cloned.1.call-update) | async-done | bytes 131088 | tf_op jit(solution)/shard_map/while/body/eval_jaxpr/psum | solution.py:57
  257.0 1.9 convolution_select_fusion.4
  258.9 2.7 constant_dynamic-slice_fusion.3
  261.6 21.0 %all-gather.16.cloned.1.call-done = f32[1024,256]{1,0:T(8,128)} async-done(((f32[128,256]{1,0:T(8,128)}), f32[1024,256]{1,0:T(8,128)}) %all-gather.16.cloned.1.call-update) | async-done | bytes 1048592 | tf_op jit(solution)/shard_map/while/body/eval_jaxpr/all_gather | solution.py:12
  284.5 3.1 select_add_fusion.2
  290.2 35.7 %all-reduce.5.cloned.1.call-done = f32[128,256]{1,0:T(8,128)} async-done(((f32[128,256]{1,0:T(8,128)}), f32[128,256]{1,0:T(8,128)}) %all-reduce.5.cloned.1.call-update) | async-done | bytes 131088 | tf_op jit(solution)/shard_map/while/body/eval_jaxpr/psum | solution.py:57
  325.9 1.9 convolution_select_fusion.4
  327.9 2.7 constant_dynamic-slice_fusion.3
  330.6 20.9 %all-gather.16.cloned.1.call-done = f32[1024,256]{1,0:T(8,128)} async-done(((f32[128,256]{1,0:T(8,128)}), f32[1024,256]{1,0:T(8,128)}) %all-gather.16.cloned.1.call-update) | async-done | bytes 1048592 | tf_op jit(solution)/shard_map/while/body/eval_jaxpr/all_gather | solution.py:12
  353.4 3.1 select_add_fusion.2
  359.1 35.7 %all-reduce.5.cloned.1.call-done = f32[128,256]{1,0:T(8,128)} async-done(((f32[128,256]{1,0:T(8,128)}), f32[128,256]{1,0:T(8,128)}) %all-reduce.5.cloned.1.call-update) | async-done | bytes 131088 | tf_op jit(solution)/shard_map/while/body/eval_jaxpr/psum | solution.py:57
  394.8 1.9 convolution_select_fusion.4
  396.8 2.7 constant_dynamic-slice_fusion.3
  399.5 20.8 %all-gather.16.cloned.1.call-done = f32[1024,256]{1,0:T(8,128)} async-done(((f32[128,256]{1,0:T(8,128)}), f32[1024,256]{1,0:T(8,128)}) %all-gather.16.cloned.1.call-update) | async-done | bytes 1048592 | tf_op jit(solution)/shard_map/while/body/eval_jaxpr/all_gather | solution.py:12
  422.3 3.1 select_add_fusion.2
  428.0 35.7 %all-reduce.5.cloned.1.call-done = f32[128,256]{1,0:T(8,128)} async-done(((f32[128,256]{1,0:T(8,128)}), f32[128,256]{1,0:T(8,128)}) %all-reduce.5.cloned.1.call-update) | async-done | bytes 131088 | tf_op jit(solution)/shard_map/while/body/eval_jaxpr/psum | solution.py:57
  465.7 2.7 constant_dynamic-slice_fusion.3
  468.4 20.8 %all-gather.16.cloned.1.call-done = f32[1024,256]{1,0:T(8,128)} async-done(((f32[128,256]{1,0:T(8,128)}), f32[1024,256]{1,0:T(8,128)}) %all-gather.16.cloned.1.call-update) | async-done | bytes 1048592 | tf_op jit(solution)/shard_map/while/body/eval_jaxpr/all_gather | solution.py:12
  491.1 3.1 select_add_fusion.2
  496.8 35.4 %all-reduce.5.cloned.1.call-done = f32[128,256]{1,0:T(8,128)} async-done(((f32[128,256]{1,0:T(8,128)}), f32[128,256]{1,0:T(8,128)}) %all-reduce.5.cloned.1.call-update) | async-done | bytes 131088 | tf_op jit(solution)/shard_map/while/body/eval_jaxpr/psum | solution.py:57
  532.2 1.9 convolution_select_fusion.4
  534.2 2.7 constant_dynamic-slice_fusion.3
  536.9 20.8 %all-gather.16.cloned.1.call-done = f32[1024,256]{1,0:T(8,128)} async-done(((f32[128,256]{1,0:T(8,128)}), f32[1024,256]{1,0:T(8,128)}) %all-gather.16.cloned.1.call-update) | async-done | bytes 1048592 | tf_op jit(solution)/shard_map/while/body/eval_jaxpr/all_gather | solution.py:12
  559.7 3.1 select_add_fusion.2
  564.0 102.6 %all-gather.10.cloned.1.call-done = f32[32,128,128]{2,1,0:T(8,128)} async-done(((f32[1,128,128]{2,1,0:T(8,128)}), f32[32,128,128]{2,1,0:T(8,128)}) %all-gather.10.cloned.1.call-update) | async-done | bytes 2097168 | tf_op jit(solution)/shard_map/all_gather | solution.py:12
  668.5 11.7 %cholesky.19 = f32[128,128]{1,0:T(8,128)S(1)} custom-call(f32[128,128]{1,0:T(8,128)S(1)} %fusion.13), custom_call_target="Cholesky" | custom-call | tf_op jit(solution)/shard_map/jit(cholesky)/cholesky | solution.py:30
  681.5 9.8 %custom-call.7 = f32[1,128,128]{1,2,0:T(8,128)S(1)} custom-call(f32[1,128,128]{2,1,0:T(8,128)S(1)} %get-tuple-element.278), custom_call_target="InvertDiagBlocksLowerTriangular" | custom-call | tf_op jit(solution)/shard_map/jit(_solve_triangular)/triangular_solve | solution.py:31
  693.1 2.6 sub.72
  696.7 2.0 gather_fusion.1
  698.7 21.4 %all-gather.12.cloned.1.call-done = f32[16,128,128]{2,1,0:T(8,128)} async-done(((f32[4,128,128]{2,1,0:T(8,128)}), f32[16,128,128]{2,1,0:T(8,128)}) %all-gather.12.cloned.1.call-update) | async-done | bytes 1048592 | tf_op jit(solution)/shard_map/all_gather | solution.py:40
  721.5 11.0 %all_gather.40 = f32[8,128,128]{2,1,0:T(8,128)} all-gather(f32[1,128,128]{2,1,0:T(8,128)S(1)} %constant_dynamic-slice_fusion.1), channel_id=1, replica_groups=mesh['prow'=8,'pcol'=4] {'prow'}, dimensions={0}, use_global_device_ids=true | all-gather | bytes 589824 | tf_op jit(solution)/shard_map/all_gather | solution.py:47
  734.1 3.4 copy_subtract_fusion
  737.5 2.9 copy.23
  740.5 4.7 all-gather.14.cloned.1.call-done
  746.5 4.7 select_select_fusion
  (106 shorter events, 55.0 us)
Async XLA Ops:
  9.5 41.0 %all-reduce.5.cloned.1.call-start = ((), (), s32[]{:S(2)}) async-start(), calls=%async_computation.4 | async-start | bytes 262144 | tf_op jit(solution)/shard_map/while/body/eval_jaxpr/psum | solution.py:57
  10.4 65.7 %all-gather.16.cloned.1.call-start = ((), (), s32[]{:S(2)}) async-start(), calls=%async_computation.5 | async-start | bytes 1179648 | tf_op jit(solution)/shard_map/while/body/eval_jaxpr/all_gather | solution.py:12
  81.2 38.3 %all-reduce.5.cloned.1.call-start = ((), (), s32[]{:S(2)}) async-start(), calls=%async_computation.4 | async-start | bytes 262144 | tf_op jit(solution)/shard_map/while/body/eval_jaxpr/psum | solution.py:57
  83.7 61.3 %all-gather.16.cloned.1.call-start = ((), (), s32[]{:S(2)}) async-start(), calls=%async_computation.5 | async-start | bytes 1179648 | tf_op jit(solution)/shard_map/while/body/eval_jaxpr/all_gather | solution.py:12
  150.1 38.0 %all-reduce.5.cloned.1.call-start = ((), (), s32[]{:S(2)}) async-start(), calls=%async_computation.4 | async-start | bytes 262144 | tf_op jit(solution)/shard_map/while/body/eval_jaxpr/psum | solution.py:57
  152.6 61.0 %all-gather.16.cloned.1.call-start = ((), (), s32[]{:S(2)}) async-start(), calls=%async_computation.5 | async-start | bytes 1179648 | tf_op jit(solution)/shard_map/while/body/eval_jaxpr/all_gather | solution.py:12
  218.6 38.3 %all-reduce.5.cloned.1.call-start = ((), (), s32[]{:S(2)}) async-start(), calls=%async_computation.4 | async-start | bytes 262144 | tf_op jit(solution)/shard_map/while/body/eval_jaxpr/psum | solution.py:57
  221.2 61.4 %all-gather.16.cloned.1.call-start = ((), (), s32[]{:S(2)}) async-start(), calls=%async_computation.5 | async-start | bytes 1179648 | tf_op jit(solution)/shard_map/while/body/eval_jaxpr/all_gather | solution.py:12
  287.7 38.3 %all-reduce.5.cloned.1.call-start = ((), (), s32[]{:S(2)}) async-start(), calls=%async_computation.4 | async-start | bytes 262144 | tf_op jit(solution)/shard_map/while/body/eval_jaxpr/psum | solution.py:57
  290.2 61.3 %all-gather.16.cloned.1.call-start = ((), (), s32[]{:S(2)}) async-start(), calls=%async_computation.5 | async-start | bytes 1179648 | tf_op jit(solution)/shard_map/while/body/eval_jaxpr/all_gather | solution.py:12
  356.5 38.3 %all-reduce.5.cloned.1.call-start = ((), (), s32[]{:S(2)}) async-start(), calls=%async_computation.4 | async-start | bytes 262144 | tf_op jit(solution)/shard_map/while/body/eval_jaxpr/psum | solution.py:57
  359.0 61.3 %all-gather.16.cloned.1.call-start = ((), (), s32[]{:S(2)}) async-start(), calls=%async_computation.5 | async-start | bytes 1179648 | tf_op jit(solution)/shard_map/while/body/eval_jaxpr/all_gather | solution.py:12
  425.4 38.3 %all-reduce.5.cloned.1.call-start = ((), (), s32[]{:S(2)}) async-start(), calls=%async_computation.4 | async-start | bytes 262144 | tf_op jit(solution)/shard_map/while/body/eval_jaxpr/psum | solution.py:57
  427.9 61.3 %all-gather.16.cloned.1.call-start = ((), (), s32[]{:S(2)}) async-start(), calls=%async_computation.5 | async-start | bytes 1179648 | tf_op jit(solution)/shard_map/while/body/eval_jaxpr/all_gather | solution.py:12
  494.3 38.0 %all-reduce.5.cloned.1.call-start = ((), (), s32[]{:S(2)}) async-start(), calls=%async_computation.4 | async-start | bytes 262144 | tf_op jit(solution)/shard_map/while/body/eval_jaxpr/psum | solution.py:57
  496.8 61.0 %all-gather.16.cloned.1.call-start = ((), (), s32[]{:S(2)}) async-start(), calls=%async_computation.5 | async-start | bytes 1179648 | tf_op jit(solution)/shard_map/while/body/eval_jaxpr/all_gather | solution.py:12
  562.8 103.9 %all-gather.10.cloned.1.call-start = ((), (), s32[]{:S(2)}) async-start(), calls=%async_computation | async-start | bytes 2162688 | tf_op jit(solution)/shard_map/all_gather | solution.py:12
  563.4 129.7 %all-reduce.3.cloned.1.call-start = ((), (), s32[]{:S(2)}) async-start(), calls=%async_computation.2 | async-start | bytes 4194304 | tf_op jit(solution)/shard_map/psum | solution.py:82
  563.4 128.3 %copy-start.1 = (f32[4,128,128]{2,1,0:T(8,128)S(1)}, f32[4,128,128]{2,1,0:T(8,128)}, u32[]{:S(2)}) copy-start(f32[4,128,128]{2,1,0:T(8,128)} %param.7) | copy-start | bytes 786436
  564.0 156.2 %all-gather.12.cloned.1.call-start = ((), (), s32[]{:S(2)}) async-start(), calls=%async_computation.1 | async-start | bytes 1310720 | tf_op jit(solution)/shard_map/all_gather | solution.py:40
  693.0 52.2 %all-gather.14.cloned.1.call-start = ((), (), s32[]{:S(2)}) async-start(), calls=%async_computation.3 | async-start | bytes 1179648 | tf_op jit(solution)/shard_map/all_gather | solution.py:12
  693.0 3.6 copy-start
Sparse Core Ops, SparseCore 0:
  13.3 37.1 all-reduce.4
  53.0 23.1 all-gather.15
  85.0 34.4 all-reduce.4
  121.8 23.1 all-gather.15
  153.6 34.4 all-reduce.4
  190.4 23.1 all-gather.15
  222.5 34.4 all-reduce.4
  259.4 23.1 all-gather.15
  291.5 34.3 all-reduce.4
  328.2 23.1 all-gather.15
  360.3 34.4 all-reduce.4
  397.1 23.1 all-gather.15
  429.2 34.4 all-reduce.4
  466.0 23.1 all-gather.15
  497.8 34.4 all-reduce.4
  534.6 23.1 all-gather.15
  566.8 89.8 all-reduce.2
  693.1 27.0 all-gather.11
  722.2 22.9 all-gather.13
Sparse Core Ops, SparseCore 1:
  566.2 100.4 all-gather.9
